TPU v7x, 128 devices: a whole 4x4x4 slice. The times are simulated.
128 devices in a mesh: row: 16 (over x, z), col: 8 (over y, core).
Axes of the slice: x: 4, y: 4, z: 4, core: 2. Of those that a mesh axis runs over, the one named last changes fastest.
Arguments:
- amplitudes: bfloat16 [16384, 16384], P('row', 'col'), may hold values from -6 to 6
- integrals: bfloat16 [16384, 4096], P('col', 'row'), may hold values from -0.046875 to 0.046875
- amp_mask: int32 [128, 128], P('row', 'col'), may hold values 0 or 1
- int_mask: int32 [128, 32], P('col', 'row'), may hold values 0 or 1
Outputs:
- ladder: bfloat16 [16384, 4096], P('row', 'col')
All inputs are finite; a program needn't handle non-finite values. No bound on the sum of `amp_mask` or of `int_mask` on one device may be relied on, other than what follows from the above.
Results may differ from a plain program's by a relative error of at most 0.001.
Values may be sent and summed in bfloat16 or wider, within the bound.
A program may use at most 128 MiB of HBM per device.

v0:
```python
import jax
import jax.numpy as jnp
from jax import lax
from jax.sharding import PartitionSpec as P

TILE = 128


def expand(mask):
    spread = jnp.repeat(jnp.repeat(mask, TILE, axis=0), TILE, axis=1)
    return spread.astype(jnp.bfloat16)


def per_device(amplitudes, integrals, amp_mask, int_mask):
    sparse_amp = amplitudes * expand(amp_mask)
    sparse_int = integrals * expand(int_mask)
    partial_value = jnp.dot(
        sparse_amp,
        lax.all_gather(sparse_int, "row", axis=1, tiled=True),
        preferred_element_type=jnp.float32,
    )
    ladder = lax.psum_scatter(partial_value, "col", scatter_dimension=1, tiled=True)
    return ladder.astype(jnp.bfloat16)


def solution(mesh):
    in_specs = (P("row", "col"), P("col", "row"), P("row", "col"), P("col", "row"))
    out_specs = P("row", "col")
    return jax.shard_map(
        per_device, mesh=mesh, in_specs=in_specs, out_specs=out_specs, check_vma=False
    )
```

profile of v0, /device:TPU:1, one launch (start us, length us, event | category | flops | bytes accessed | tf_op | source)
XLA Modules:
  0.0 265.9 jit_solution(4168106295409174461)
XLA Ops:
  6.5 0.0 copy-start
  6.5 0.0 all-gather.2.cloned.1.call-start
  6.5 0.7 convert_element_type.28
  7.2 0.1 copy.5
  7.3 0.1 broadcast_in_dim.14
  7.4 5.8 %broadcast_in_dim.15 = bf16[2048,2,128]{2,1,0:T(2,128)(2,1)S(1)} broadcast(bf16[2048,2]{1,0:T(8,128)(2,1)S(1)} %bitcast.12), dimensions={0,1} | broadcast | bytes 1056768 | tf_op jit(solution)/shard_map/broadcast_in_dim | solution.py:10
  13.2 2.4 bitcast_multiply_fusion.2
  15.6 0.0 all-gather.2.cloned.1.call-update
  15.6 0.0 reduce-scatter.2.cloned.1.call-start
  15.6 0.0 copy-done
  15.7 121.9 %all-gather.2.cloned.1.call-done = bf16[2048,4096]{1,0:T(8,128)(2,1)} async-done(((bf16[2048,256]{1,0:T(8,128)(2,1)}), bf16[2048,4096]{1,0:T(8,128)(2,1)}) %all-gather.2.cloned.1.call-update) | async-done | bytes 16777232 | tf_op jit(solution)/shard_map/all_gather | solution.py:19
  137.5 0.0 copy-start.1
  137.6 4.5 %broadcast_in_dim.13 = bf16[1024,16,128]{2,1,0:T(8,128)(2,1)S(1)} broadcast(bf16[1024,16]{1,0:T(8,128)(2,1)S(1)} %bitcast.13), dimensions={0,1} | broadcast | bytes 4227072 | tf_op jit(solution)/shard_map/broadcast_in_dim | solution.py:10
  142.1 0.0 copy-done.1
  142.1 22.2 %fusion = f32[1024,4096]{1,0:T(8,128)} fusion(bf16[2048,4096]{1,0:T(8,128)(2,1)} %all-gather.2.cloned.1.call-done, bf16[1024,2048]{1,0:T(8,128)(2,1)S(1)} %copy-done.1, bf16[128,8,16,128]{3,2,1,0:T(8,128)(2,1)S(1)} %bitcast.11), kind=kOutput, calls=%fused_computation.1 | convolution fusion | flops 17181966336 | bytes 41943040 | tf_op jit(solution)/shard_map/dot_general | solution.py:17
  164.3 0.0 reduce-scatter.2.cloned.1.call-update
  164.3 92.0 %reduce-scatter.2.cloned.1.call-done = f32[1024,512]{1,0:T(8,128)} async-done(((f32[1024,4096]{1,0:T(8,128)}), f32[1024,512]{1,0:T(8,128)}) %reduce-scatter.2.cloned.1.call-update) | async-done | bytes 2097168 | tf_op jit(solution)/shard_map/reduce_scatter | solution.py:22
  256.3 2.7 %convert_element_type.31 = bf16[1024,512]{1,0:T(8,128)(2,1)} convert(f32[1024,512]{1,0:T(8,128)} %reduce-scatter.2.cloned.1.call-done) | non-fusion elementwise | flops 524288 | bytes 3145728 | tf_op jit(solution)/shard_map/convert_element_type | solution.py:23
  (2 shorter events, 0.0 us)
Async XLA Ops:
  6.5 9.1 %copy-start = (s32[8,16]{1,0:T(8,128)S(1)}, s32[8,16]{1,0:T(8,128)}, u32[]{:S(2)}) copy-start(s32[8,16]{1,0:T(8,128)} %param.6) | copy-start | bytes 1540
  6.5 131.0 %all-gather.2.cloned.1.call-start = ((), (), s32[]{:S(2)}) async-start(), calls=%async_computation.1 | async-start | bytes 17825792 | tf_op jit(solution)/shard_map/all_gather | solution.py:19
  15.6 240.8 %reduce-scatter.2.cloned.1.call-start = ((), (), s32[]{:S(2)}) async-start(), calls=%async_computation.2 | async-start | bytes 18874368 | tf_op jit(solution)/shard_map/reduce_scatter | solution.py:22
  137.5 4.5 %copy-start.1 = (bf16[1024,2048]{1,0:T(8,128)(2,1)S(1)}, bf16[1024,2048]{1,0:T(8,128)(2,1)}, u32[]{:S(2)}) copy-start(bf16[1024,2048]{1,0:T(8,128)(2,1)} %param.4) | copy-start | bytes 12582916
Sparse Core Ops, SparseCore 0:
  15.7 121.7 all-gather.1
  164.5 91.8 reduce-scatter.1
where the time goes:
time: 266 us
  waiting for transfers between devices  214 us (80%)
  matrix products  22.2 us (8%)
  between operations  13.4 us (5%)
  local copies, waits for them, and re-layouts  10.5 us (4%)
  other arithmetic  5.77 us (2%)
    all_gather x1, waiting for transfers between devices, per_device(): lax.all_gather(sparse_int, 'row', axis=1, tiled=True)  122 us
    reduce_scatter x1, waiting for transfers between devices, per_device(): lax.psum_scatter(partial_value, 'col', scatter_dimension=1, tiled=True)  92 us
    dot_general x1, matrix products, per_device(): jnp.dot(sparse_amp, lax.all_gather(sparse_int, 'row', axis=1, tiled=True)...  22.2 us
    broadcast_in_dim x4, local copies, waits for them, and re-layouts, expand(): spread = jnp.repeat(jnp.repeat(mask, TILE, axis=0), TILE, axis=1)  10.4 us
  transfers between devices with their start and end apart: 2, of which 2 were waited for; matrix products, arithmetic and copies ran while one was open for 0% of the time, Pallas kernels for 0%

commit v1 on v0

--- a/solution.py
+++ b/solution.py
@@ -16,7 +16,9 @@
     sparse_int = integrals * expand(int_mask)
     partial_value = jnp.dot(
         sparse_amp,
-        lax.all_gather(sparse_int, "row", axis=1, tiled=True),
+        jnp.concatenate(
+            lax.all_to_all(jnp.stack([sparse_int] * lax.axis_size("row")), "row", 0, 0), axis=1
+        ),
         preferred_element_type=jnp.float32,
     )
     ladder = lax.psum_scatter(partial_value, "col", scatter_dimension=1, tiled=True)

time: 266 us -> 457 us (1.72)
  waiting for transfers between devices: 214 us -> 391 us
  starting transfers between devices: 0.04 us -> 8.64 us
  local copies, waits for them, and re-layouts: 10.5 us -> 17.1 us
    all_to_all x0 -> x1, waiting for transfers between devices: none -> 293 us  [per_device(): lax.all_to_all(jnp.stack([sparse_int] * lax.axis_size('row')), 'row', 0, 0)]
    all_gather x1 -> x0, waiting for transfers between devices: 122 us -> none  [per_device(): lax.all_gather(sparse_int, 'row', axis=1, tiled=True)]
    all_to_all x0 -> x1, starting transfers between devices: none -> 8.6 us  [per_device(): lax.all_to_all(jnp.stack([sparse_int] * lax.axis_size('row')), 'row', 0, 0)]
    another operation x0 -> x1, local copies, waits for them, and re-layouts: none -> 5.97 us  [per_device(): jnp.stack([sparse_int] * lax.axis_size('row'))]
    reduce_scatter x1, waiting for transfers between devices: 92 us -> 97.3 us  [per_device(): lax.psum_scatter(partial_value, 'col', scatter_dimension=1, tiled=True)]
where the time goes in v1:
time: 457 us
  waiting for transfers between devices  391 us (86%)
  matrix products  22.4 us (5%)
  local copies, waits for them, and re-layouts  17.1 us (4%)
  between operations  13.5 us (3%)
  starting transfers between devices  8.64 us (2%)
  other arithmetic  4.79 us (1%)
    all_to_all x1, waiting for transfers between devices, per_device(): lax.all_to_all(jnp.stack([sparse_int] * lax.axis_size('row')), 'row', 0, 0)  293 us
    reduce_scatter x1, waiting for transfers between devices, per_device(): lax.psum_scatter(partial_value, 'col', scatter_dimension=1, tiled=True)  97.3 us
    dot_general x1, matrix products, per_device(): jnp.dot(sparse_amp, jnp.concatenate(lax.all_to_all(jnp.stack([sparse_int]...  22.4 us
    broadcast_in_dim x4, local copies, waits for them, and re-layouts, expand(): spread = jnp.repeat(jnp.repeat(mask, TILE, axis=0), TILE, axis=1)  10.4 us
  transfers between devices with their start and end apart: 2, of which 2 were waited for; matrix products, arithmetic and copies ran while one was open for 0% of the time, Pallas kernels for 0%

profile of v1, /device:TPU:1, one launch (start us, length us, event | category | flops | bytes accessed | tf_op | source)
XLA Modules:
  0.0 457.0 jit_solution(6361364830935335135)
XLA Ops:
  6.5 0.7 convert_element_type.28
  7.2 0.1 copy.6
  7.3 0.1 broadcast_in_dim.14
  7.4 5.8 %broadcast_in_dim.15 = bf16[2048,2,128]{2,1,0:T(2,128)(2,1)S(1)} broadcast(bf16[2048,2]{1,0:T(8,128)(2,1)S(1)} %bitcast.15), dimensions={0,1} | broadcast | bytes 1056768 | tf_op jit(solution)/shard_map/broadcast_in_dim | solution.py:10
  13.2 1.4 bitcast_multiply_fusion.2
  14.6 0.6 copy.7
  15.2 6.0 %stack.2 = bf16[16,2048,256]{1,2,0:T(8,128)(2,1)} broadcast(bf16[2048,256]{0,1:T(8,128)(2,1)S(1)} %copy.7), dimensions={1,2} | broadcast | bytes 17825792 | tf_op jit(solution)/shard_map/stack | solution.py:20
  21.2 0.0 copy-start
  21.2 8.6 %all-to-all-start = ((bf16[16,2048,256]{1,2,0:T(8,128)(2,1)}), bf16[16,2048,256]{1,2,0:T(8,128)(2,1)}, u32[]{:S(2)}, u32[]{:S(2)}) async-start(bf16[16,2048,256]{1,2,0:T(8,128)(2,1)} %stack.2), calls=%async_computation | async-start | bytes 33554432 | tf_op jit(solution)/shard_map/all_to_all | solution.py:20
  29.8 0.0 reduce-scatter.2.cloned.1.call-start
  29.9 0.0 copy-done
  29.9 293.2 %all-to-all-done = bf16[16,2048,256]{1,2,0:T(8,128)(2,1)} async-done(((bf16[16,2048,256]{1,2,0:T(8,128)(2,1)}), bf16[16,2048,256]{1,2,0:T(8,128)(2,1)}, u32[]{:S(2)}, u32[]{:S(2)}) %all-to-all-start) | async-done | bytes 16777248 | tf_op jit(solution)/shard_map/all_to_all | solution.py:20
  323.1 0.0 copy-start.1
  323.2 4.5 broadcast_in_dim.13
  327.6 0.0 copy-done.1
  327.7 22.4 %fusion = f32[1024,4096]{1,0:T(8,128)} fusion(bf16[2048,4096]{0,1:T(8,128)(2,1)} %bitcast.3, bf16[1024,2048]{1,0:T(8,128)(2,1)S(1)} %copy-done.1, bf16[128,8,16,128]{3,2,1,0:T(8,128)(2,1)S(1)} %bitcast.14), kind=kOutput, calls=%fused_computation.1 | convolution fusion | flops 17181966336 | bytes 41943040 | tf_op jit(solution)/shard_map/dot_general | solution.py:17
  350.1 0.0 reduce-scatter.2.cloned.1.call-update
  350.1 97.3 %reduce-scatter.2.cloned.1.call-done = f32[1024,512]{1,0:T(8,128)} async-done(((f32[1024,4096]{1,0:T(8,128)}), f32[1024,512]{1,0:T(8,128)}) %reduce-scatter.2.cloned.1.call-update) | async-done | bytes 2097168 | tf_op jit(solution)/shard_map/reduce_scatter | solution.py:24
  447.4 2.7 convert_element_type.31
  (2 shorter events, 0.0 us)
Async XLA Ops:
  21.2 8.7 %copy-start = (s32[8,16]{1,0:T(8,128)S(1)}, s32[8,16]{1,0:T(8,128)}, u32[]{:S(2)}) copy-start(s32[8,16]{1,0:T(8,128)} %param.6) | copy-start | bytes 1540
  21.2 301.9 %all-to-all-start = ((bf16[16,2048,256]{1,2,0:T(8,128)(2,1)}), bf16[16,2048,256]{1,2,0:T(8,128)(2,1)}, u32[]{:S(2)}, u32[]{:S(2)}) async-start(bf16[16,2048,256]{1,2,0:T(8,128)(2,1)} %stack.2), calls=%async_computation | async-start | bytes 33554432 | tf_op jit(solution)/shard_map/all_to_all | solution.py:20
  29.8 417.6 %reduce-scatter.2.cloned.1.call-start = ((), (), s32[]{:S(2)}) async-start(), calls=%async_computation.2 | async-start | bytes 18874368 | tf_op jit(solution)/shard_map/reduce_scatter | solution.py:24
  323.1 4.5 copy-start.1
Sparse Core Ops, SparseCore 0:
  350.2 97.1 reduce-scatter.1
